TPU v7x, 32 devices: a whole 2x2x4 slice. The times are simulated.
32 devices in a mesh: seq: 8 (over z, y), head: 4 (over x, core).
Axes of the slice: x: 2, y: 2, z: 4, core: 2. Of those that a mesh axis runs over, the one named last changes fastest.
Arguments:
- routed_qkv: bfloat16 [3, 2048, 1024], P(None, 'seq', 'head'), may hold values from -64 to 64
- local_qkv: bfloat16 [3, 2048, 3072], P(None, 'seq', 'head'), may hold values from -64 to 64
- cluster_ids: int32 [8, 2048, 1], P('head', 'seq'), may hold values from 0 to 15; in each aligned block of 256 rows (0 to 255, 256 to 511, ..., all dimensions but the last counted through in order) at most 32 rows name the same one
- wo_routed: bfloat16 [1024, 4096], P('head', 'seq'), may hold values from -0.09375 to 0.09375
- wo_local: bfloat16 [3072, 4096], P('head', 'seq'), may hold values from -0.09375 to 0.09375
Outputs:
- layer_out: bfloat16 [2048, 4096], P('seq', 'head')
Inputs may be any that keep to these rules, and one draw needn't show every extreme that they name: `cluster_ids`: in each routed head, no cluster holds more than 32 of the 256 tokens of one index of seq (aligned blocks of 256 rows), and some cluster holds exactly 32 of them.
All inputs are finite; a program needn't handle non-finite values.
Results may differ from a plain program's by a relative error of at most 0.0095.
Values may be sent and summed in bfloat16 or wider, within the bound.
No kernel may reach another device: no remote copies, remote signals or barrier semaphores. Data moves between devices by JAX's collectives and lax.ppermute only.
A program may use at most 64 MiB of HBM per device.

v0:
```python
import math

import jax
import jax.numpy as jnp
from jax import lax
from jax.experimental import pallas as pl
from jax.experimental.pallas import tpu as pltpu
from jax.sharding import PartitionSpec as P


HD = 128
WIN = 256
CL_DEV = 2
LOW = -1e30
SCALE = 1.0 / math.sqrt(HD)


def shifted(block, axis, distance):
    devices = range(lax.axis_size(axis))
    route = [(i - distance, i) for i in devices if i - distance in devices]
    return lax.ppermute(block, axis, route)


def attend(query, keys, values, allowed):
    scores = jnp.einsum("...qd,...kd->...qk", query, keys, preferred_element_type=jnp.float32) * (
        1.0 / math.sqrt(HD)
    )
    scores = jnp.where(allowed, scores, jnp.float32(-1e30))
    largest = jnp.max(scores, axis=-1, keepdims=True)
    raised = jnp.exp(scores - largest)
    weights = (raised / jnp.sum(raised, axis=-1, keepdims=True)).astype(jnp.bfloat16)
    return jnp.einsum(
        "...qk,...kd->...qd", weights, values, preferred_element_type=jnp.float32
    ).astype(jnp.bfloat16)


def general(routed_qkv, local_qkv, cluster_ids, wo_routed, wo_local):
    seq_count = lax.axis_size("seq")
    seq_place = lax.axis_index("seq")
    tok_rows = routed_qkv.shape[1]
    routed_count = cluster_ids.shape[0]
    local_count = local_qkv.shape[2] // HD
    cluster_total = CL_DEV * seq_count
    most_slots = max(2, 2 * tok_rows // cluster_total)
    proj_rows = jnp.concatenate([wo_routed, wo_local], axis=0)
    head_rows = (
        routed_qkv.reshape(3, tok_rows, routed_count, HD)
        .transpose(2, 1, 0, 3)
        .reshape(routed_count, tok_rows, 3 * HD)
    )
    cluster = cluster_ids[:, :, 0]
    labels = jnp.arange(cluster_total, dtype=jnp.int32)
    onehot = (cluster[:, :, None] == labels[None, None, :]).astype(jnp.int32)
    rank = jnp.sum((jnp.cumsum(onehot, axis=1) - 1) * onehot, axis=2)
    slot_index = cluster * most_slots + rank
    own_pos = seq_place * tok_rows + jnp.arange(tok_rows, dtype=jnp.int32)
    slot_total = cluster_total * most_slots

    def place_rows(slot_row, data):
        return jnp.zeros((slot_total, 3 * HD), data.dtype).at[slot_row].set(data)

    def place_pos(slot_row):
        return jnp.full((slot_total,), -1, jnp.int32).at[slot_row].set(own_pos)

    send_rows = jax.vmap(place_rows)(slot_index, head_rows)
    send_pos = jax.vmap(place_pos)(slot_index)
    rows = lax.all_to_all(send_rows, "seq", split_axis=1, concat_axis=1, tiled=True)
    positions = lax.all_to_all(send_pos, "seq", split_axis=1, concat_axis=1, tiled=True)
    count = rows.shape[0]
    slots = rows.shape[1]
    group = seq_count * most_slots
    members = (
        rows.reshape(count, seq_count, CL_DEV, most_slots, 3 * HD)
        .transpose(0, 2, 1, 3, 4)
        .reshape(count, CL_DEV, group, 3 * HD)
    )
    where_at = (
        positions.reshape(count, seq_count, CL_DEV, most_slots)
        .transpose(0, 2, 1, 3)
        .reshape(count, CL_DEV, group)
    )
    allowed = (where_at[..., None, :] >= 0) & (where_at[..., None, :] <= where_at[..., :, None])
    result = attend(members[..., :HD], members[..., HD : 2 * HD], members[..., 2 * HD :], allowed)
    answered = (
        result.reshape(count, CL_DEV, seq_count, most_slots, HD)
        .transpose(0, 2, 1, 3, 4)
        .reshape(count, slots, HD)
    )
    returned = lax.all_to_all(answered, "seq", split_axis=1, concat_axis=1, tiled=True)
    picked = jnp.take_along_axis(returned, slot_index[:, :, None], axis=1)
    routed_attn = picked.transpose(1, 0, 2).reshape(tok_rows, routed_count * HD)
    heads = local_qkv.reshape(3, tok_rows, local_count, HD).transpose(0, 2, 1, 3)
    tail = jnp.stack([heads[1], heads[2]])
    earlier = shifted(tail, "seq", 1)
    keys = jnp.concatenate([earlier[0], heads[1]], axis=1)
    values = jnp.concatenate([earlier[1], heads[2]], axis=1)
    key_pos = seq_place * tok_rows - WIN + jnp.arange(WIN + tok_rows, dtype=jnp.int32)
    query_pos = seq_place * tok_rows + jnp.arange(tok_rows, dtype=jnp.int32)
    allowed = (
        (key_pos[None, :] >= 0)
        & (key_pos[None, :] <= query_pos[:, None])
        & (key_pos[None, :] > query_pos[:, None] - WIN)
    )
    result = attend(heads[0], keys, values, allowed[None])
    local_attn = result.transpose(1, 0, 2).reshape(tok_rows, local_count * HD)
    joined = jnp.concatenate([routed_attn, local_attn], axis=1)
    terms = jnp.dot(
        joined,
        lax.all_gather(proj_rows, "seq", axis=1, tiled=True),
        preferred_element_type=jnp.float32,
    )
    rounded = terms.astype(jnp.bfloat16)
    return (
        lax.psum_scatter(rounded, "head", scatter_dimension=1, tiled=True)
        .astype(jnp.float32)
        .astype(jnp.bfloat16)
    )


AXES = ("seq", "head")


def split_seq(place):
    return place // 4, (place // 2) % 2, place % 2


def moved(block, target):
    route = []
    for place in range(8):
        for head in range(4):
            to = target(place, head)
            if to is not None:
                route.append((place * 4 + head, to[0] * 4 + to[1]))
    return lax.ppermute(block, AXES, route)


def nt(a, b):
    return lax.dot_general(a, b, (((1,), (1,)), ((), ())), preferred_element_type=jnp.float32)


def window_body(first, qkv, tail, out):
    rows = out.shape[0]
    row = lax.broadcasted_iota(jnp.int32, (rows, rows), 0)
    col = lax.broadcasted_iota(jnp.int32, (rows, rows), 1)
    ahead = col - row
    start = first[0]
    for i in range(out.shape[1] // HD):
        at = slice(i * HD, (i + 1) * HD)
        query = qkv[0, :, at]
        later = jnp.where(ahead <= 0, nt(query, qkv[1, :, at]) * SCALE, LOW)
        earlier = jnp.where(ahead > start, nt(query, tail[0, :, at]) * SCALE, LOW)
        top = jnp.max(jnp.maximum(later, earlier), axis=1, keepdims=True)
        later = jnp.exp(later - top)
        earlier = jnp.exp(earlier - top)
        total = jnp.sum(later + earlier, axis=1, keepdims=True)
        mixed = jnp.dot(
            later.astype(jnp.bfloat16), qkv[2, :, at], preferred_element_type=jnp.float32
        ) + jnp.dot(
            earlier.astype(jnp.bfloat16), tail[1, :, at], preferred_element_type=jnp.float32
        )
        out[:, at] = (mixed / total).astype(out.dtype)


WHOLE = pl.BlockSpec(memory_space=pltpu.VMEM)
SCALARS = pl.BlockSpec(memory_space=pltpu.SMEM)


def window_heads(local_qkv, tail, is_first):
    rows, width = local_qkv.shape[1:]
    first = jnp.where(is_first, rows, 0).astype(jnp.int32).reshape(1)
    return pl.pallas_call(
        window_body,
        in_specs=[SCALARS] + [WHOLE] * 2,
        out_specs=WHOLE,
        out_shape=jax.ShapeDtypeStruct((rows, width), jnp.bfloat16),
        compiler_params=pltpu.CompilerParams(vmem_limit_bytes=12 << 20),
        name="window_heads",
    )(first, local_qkv, tail)


def names_of(ref, at, e, rows):
    two = ref[at : at + 16, e * HD : (e + 1) * HD].astype(jnp.float32)
    turned = jnp.transpose(two)
    along = jnp.concatenate([two[i : i + 1] for i in range(rows // HD)], axis=1)
    down = jnp.concatenate([turned[:, i : i + 1] for i in range(rows // HD)], axis=0)
    return along, down


def near_body(shift, *refs):
    near, (acc, stat, scores, values) = refs[:4], refs[4:]
    rows = acc.shape[1]
    row = lax.broadcasted_iota(jnp.int32, (rows, rows), 0)
    col = lax.broadcasted_iota(jnp.int32, (rows, rows), 1)
    gap = row - col
    for e in range(acc.shape[2] // HD):
        at = slice(e * HD, (e + 1) * HD)
        names = [names_of(ref, 3 * rows, e, rows) for ref in near]
        for j in range(4):
            values[j * rows : (j + 1) * rows] = near[j][2 * rows : 3 * rows, at]
        for i in range(4):
            query = near[i][0:rows, at]
            for j in range(4):
                allowed = (gap >= shift[i * 4 + j]) & (names[i][1] == names[j][0])
                part = nt(query, near[j][rows : 2 * rows, at]) * SCALE
                scores[:, j * rows : (j + 1) * rows] = jnp.where(allowed, part, LOW)
            raised = scores[...]
            top = jnp.max(raised, axis=1, keepdims=True)
            raised = jnp.exp(raised - top)
            stat[i, :, 2 * e : 2 * e + 1] = top
            stat[i, :, 2 * e + 1 : 2 * e + 2] = jnp.sum(raised, axis=1, keepdims=True)
            acc[i, :, at] = jnp.dot(
                raised.astype(jnp.bfloat16), values[...], preferred_element_type=jnp.float32
            )


def past_body(half, *refs):
    near, past, (acc, stat, out, scores, values) = refs[:4], refs[4:8], refs[8:]
    rows = out.shape[1]

    @pl.when(half[0] == 0)
    def _():
        for e in range(out.shape[2] // HD):
            at = slice(e * HD, (e + 1) * HD)
            for i in range(4):
                total = stat[i, :, 2 * e + 1 : 2 * e + 2]
                out[i, :, at] = (acc[i, :, at] / total).astype(out.dtype)

    @pl.when(half[0] == 1)
    def _():
        for e in range(out.shape[2] // HD):
            at = slice(e * HD, (e + 1) * HD)
            downs = [names_of(ref, 3 * rows, e, rows)[1] for ref in near]
            alongs = [names_of(ref, 2 * rows, e, rows)[0] for ref in past]
            for j in range(4):
                values[j * rows : (j + 1) * rows] = past[j][rows : 2 * rows, at]
            for i in range(4):
                query = near[i][0:rows, at]
                for j in range(4):
                    part = nt(query, past[j][0:rows, at]) * SCALE
                    scores[:, j * rows : (j + 1) * rows] = jnp.where(
                        downs[i] == alongs[j], part, LOW
                    )
                raised = scores[...]
                before = stat[i, :, 2 * e : 2 * e + 1]
                top = jnp.maximum(before, jnp.max(raised, axis=1, keepdims=True))
                raised = jnp.exp(raised - top)
                scaled = jnp.exp(before - top)
                total = scaled * stat[i, :, 2 * e + 1 : 2 * e + 2] + jnp.sum(
                    raised, axis=1, keepdims=True
                )
                mixed = scaled * acc[i, :, at] + jnp.dot(
                    raised.astype(jnp.bfloat16), values[...], preferred_element_type=jnp.float32
                )
                out[i, :, at] = (mixed / total).astype(out.dtype)


def routed_near(near, within, rows):
    blocks = jnp.array([0, 2, 1, 3], jnp.int32) ^ within
    shift = ((blocks[None, :] - blocks[:, None]) * rows).reshape(16).astype(jnp.int32)
    cols = near[0].shape[1]
    return pl.pallas_call(
        near_body,
        in_specs=[SCALARS] + [WHOLE] * 4,
        out_specs=(WHOLE, WHOLE),
        out_shape=(
            jax.ShapeDtypeStruct((4, rows, cols), jnp.float32),
            jax.ShapeDtypeStruct((4, rows, HD), jnp.float32),
        ),
        scratch_shapes=[
            pltpu.VMEM((rows, 4 * rows), jnp.float32),
            pltpu.VMEM((4 * rows, HD), jnp.bfloat16),
        ],
        compiler_params=pltpu.CompilerParams(vmem_limit_bytes=20 << 20),
        name="routed_near",
    )(shift, *near)


def routed_past(half, near, past, acc, stat):
    rows, cols = acc.shape[1:]
    return pl.pallas_call(
        past_body,
        in_specs=[SCALARS] + [WHOLE] * 10,
        out_specs=WHOLE,
        out_shape=jax.ShapeDtypeStruct((4, rows, cols), jnp.bfloat16),
        scratch_shapes=[
            pltpu.VMEM((rows, 4 * rows), jnp.float32),
            pltpu.VMEM((4 * rows, HD), jnp.bfloat16),
        ],
        compiler_params=pltpu.CompilerParams(vmem_limit_bytes=20 << 20),
        name="routed_past",
    )(half.astype(jnp.int32).reshape(1), *near, *past, acc, stat)


def project_body(use, routed, l0, l1, l2, l3, wr0, wl0, wr1, *rest):
    *others, keep, send = rest
    width = wr0.shape[1]
    part = others[0].shape[0]

    def product(a, b):
        return jnp.dot(a, b, preferred_element_type=jnp.float32)

    def fill(slot, local, out):
        mine = product(routed[slot], wr0[...]) + product(local[...], wl0[...])
        out[:, 0:width] = mine.astype(out.dtype)
        theirs = product(routed[slot], wr1[...])
        for i, other in enumerate(others):
            theirs = theirs + product(local[:, i * part : (i + 1) * part], other[...])
        out[:, width:] = theirs.astype(out.dtype)

    for slot, local in enumerate((l0, l1, l2, l3)):

        @pl.when(use[slot] == 1)
        def _(slot=slot, local=local):
            fill(slot, local, keep)

        @pl.when(use[slot] == 2)
        def _(slot=slot, local=local):
            fill(slot, local, send)


def project(use, routed, local, weights):
    shape = jax.ShapeDtypeStruct((routed.shape[1], 2 * weights[0].shape[1]), jnp.bfloat16)
    return pl.pallas_call(
        project_body,
        in_specs=[SCALARS] + [WHOLE] * (5 + len(weights)),
        out_specs=(WHOLE, WHOLE),
        out_shape=(shape, shape),
        compiler_params=pltpu.CompilerParams(vmem_limit_bytes=24 << 20),
        name="project",
    )(use, routed, *local, *weights)


def block_of_32(routed_qkv, local_qkv, cluster_ids, wo_routed, wo_local):
    place = lax.axis_index("seq")
    head = lax.axis_index("head")
    half, mid, low = split_seq(place)
    far, core = head // 2, head % 2
    rows = routed_qkv.shape[1]
    cols = routed_qkv.shape[2]

    def swap(block, bit):
        return moved(block, lambda s, h: (s ^ bit, h))

    def swap_upper(block, bit):
        return moved(block, lambda s, h: (s ^ bit, h) if s >= 4 else None)

    tail = moved(local_qkv[1:], lambda s, h: (s + 1, h) if s < 7 else None)
    names = cluster_ids.reshape(cols // HD, rows // HD, HD).transpose(1, 0, 2).reshape(rows // HD, cols)
    names = jnp.pad(names.astype(jnp.bfloat16), ((0, 16 - rows // HD), (0, 0)))
    own = jnp.concatenate([routed_qkv.reshape(3 * rows, cols), names], axis=0)
    crossed = moved(own[rows:], lambda s, h: (s + 4, h) if s < 4 else None)
    near_mid = swap(own, 2)
    past_mid = swap_upper(crossed, 2)
    past_low = swap_upper(crossed, 1)
    part = routed_qkv.shape[2]
    others = [
        swap(wo_local[i * part : (i + 1) * part], 4)
        for i in range(wo_local.shape[0] // part)
    ]
    other_routed = swap(wo_routed, 4)
    near_both = swap(near_mid, 1)
    near_low = swap(own, 1)
    result = window_heads(local_qkv, tail, place == 0)
    local_mid = swap(result, 2)
    local_low = swap(result, 1)
    past_both = swap_upper(past_mid, 1)
    local_both = swap(local_mid, 1)
    near = (own, near_mid, near_low, near_both)
    past = (crossed, past_mid, past_low, past_both)
    local = (result, local_mid, local_low, local_both)
    acc, stat = routed_near(near, place % 4, rows)
    routed = routed_past(half, near, past, acc, stat)

    slots = jnp.array([0, 2, 1, 3], jnp.int32)
    kept = jnp.where(slots % 2 == low ^ core, 1, 2)
    weights = (wo_routed, wo_local, other_routed, *others)
    here = half == far

    def target(flip):
        def to(s, h):
            r, z, y = split_seq(s)
            return r * 4 + (z ^ y ^ flip) * 2 + h % 2, (h // 2) * 2 + z

        return to

    done = []
    for flip in range(2):
        use = jnp.where(slots // 2 == low ^ flip, kept, 0).astype(jnp.int32)
        keep, send = project(use, routed, local, weights)
        got = moved(send, lambda s, h: (s, h ^ 1))
        both = keep.astype(jnp.float32) + got.astype(jnp.float32)
        width = both.shape[1] // 2
        mine = jnp.where(here, both[:, :width], both[:, width:])
        theirs = jnp.where(here, both[:, width:], both[:, :width]).astype(jnp.bfloat16)
        total = mine + moved(theirs, lambda s, h: (s, h ^ 2)).astype(jnp.float32)
        done.append(moved(total.astype(jnp.bfloat16), target(flip)))
    ahead = mid == core
    return jnp.concatenate(
        [jnp.where(ahead, done[0], done[1]), jnp.where(ahead, done[1], done[0])], axis=1
    )


def on_device(*arrays):
    if lax.axis_size("seq") == 8 and lax.axis_size("head") == 4:
        return block_of_32(*arrays)
    return general(*arrays)


def solution(mesh):
    placed = (
        P(None, "seq", "head"),
        P(None, "seq", "head"),
        P("head", "seq", None),
        P("head", "seq"),
        P("head", "seq"),
    )
    return jax.shard_map(
        on_device, mesh=mesh, in_specs=placed, out_specs=P("seq", "head"), check_vma=False
    )
```

profile of v0, /device:TPU:26, one launch (start us, length us, event | category | flops | bytes accessed | tf_op | source)
XLA Modules:
  0.0 127.7 jit_solution(16198234257107595326)
XLA Ops:
  0.0 2.2 %slice.32 = bf16[2,256,768]{2,1,0:T(8,128)(2,1)} slice(bf16[3,256,768]{2,1,0:T(8,128)(2,1)} %qkv.1), slice={[1:3], [0:256], [0:768]} | slice | bytes 1572864 | tf_op jit(solution)/shard_map/slice | solution.py:347
  2.2 3.4 %collective-permute-start.7 = (bf16[2,256,768]{2,1,0:T(8,128)(2,1)}, bf16[2,256,768]{2,1,0:T(8,128)(2,1)}, u32[]{:S(2)}, u32[]{:S(2)}) collective-permute-start(bf16[2,256,768]{2,1,0:T(8,128)(2,1)} %slice.32), channel_id=1, source_target_pairs={{0,4},{1,5},{2,6},{3,7},{4,8},{5,9},{6,10},{7,11},{8,12},{9,13},{1... | collective-permute-start | bytes 2359304 | tf_op jit(solution)/shard_map/ppermute | solution.py:134
  7.7 14.8 %collective-permute-done.3.refs_4_ = bf16[528,256]{1,0:T(8,128)(2,1)} collective-permute-done((bf16[528,256]{1,0:T(8,128)(2,1)S(1)}, bf16[528,256]{1,0:T(8,128)(2,1)}, u32[]{:S(2)}, u32[]{:S(2)}) %collective-permute-start.3) | collective-permute-done | bytes 270368 | tf_op jit(solution)/shard_map/ppermute | solution.py:134
  22.5 1.9 %collective-permute-start.4 = (bf16[528,256]{1,0:T(8,128)(2,1)}, bf16[528,256]{1,0:T(8,128)(2,1)}, u32[]{:S(2)}, u32[]{:S(2)}) collective-permute-start(bf16[528,256]{1,0:T(8,128)(2,1)} %collective-permute-done.3.refs_4_), channel_id=1, source_target_pairs={{16,24},{17,25},{18,26},{19,27},{20,28},{21,29},{22,30},{23,31},{2... | collective-permute-start | bytes 811016 | tf_op jit(solution)/shard_map/ppermute | solution.py:134
  25.3 14.2 %collective-permute-start.1 = (bf16[784,256]{1,0:T(8,128)(2,1)S(1)}, bf16[784,256]{1,0:T(8,128)(2,1)}, u32[]{:S(2)}, u32[]{:S(2)}) collective-permute-start(bf16[784,256]{1,0:T(8,128)(2,1)S(1)} %fusion.1.refs_0_), channel_id=1, source_target_pairs={{0,4},{1,5},{2,6},{3,7},{4,0},{5,1},{6,2},{7,3},{8,12},{9,13},{10,... | collective-permute-start | bytes 1204232 | tf_op jit(solution)/shard_map/ppermute | solution.py:134
  39.6 3.2 %window_heads.1.l0 = bf16[256,768]{1,0:T(8,128)(2,1)S(1)} custom-call(s32[1]{0:T(128)} %bitcast.3.first, bf16[3,256,768]{2,1,0:T(8,128)(2,1)S(1)} %copy-done.1, bf16[2,256,768]{2,1,0:T(8,128)(2,1)} %collective-permute-done.7.tail), custom_call_target="tpu_custom_call" | custom-call | tf_op jit(solution)/shard_map/window_heads/pallas_call | solution.py:171
  42.8 2.1 %collective-permute-start.8 = (bf16[256,768]{1,0:T(8,128)(2,1)S(1)}, bf16[256,768]{1,0:T(8,128)(2,1)S(1)}, u32[]{:S(2)}, u32[]{:S(2)}) collective-permute-start(bf16[256,768]{1,0:T(8,128)(2,1)S(1)} %window_heads.1.l0), channel_id=1, source_target_pairs={{0,8},{1,9},{2,10},{3,11},{4,12},{5,13},{6,14},{7,15},{8,0},{9,1},... | collective-permute-start | bytes 1179656 | tf_op jit(solution)/shard_map/ppermute | solution.py:134
  44.9 10.6 %collective-permute-start.5 = (bf16[528,256]{1,0:T(8,128)(2,1)}, bf16[528,256]{1,0:T(8,128)(2,1)S(1)}, u32[]{:S(2)}, u32[]{:S(2)}) collective-permute-start(bf16[528,256]{1,0:T(8,128)(2,1)} %collective-permute-done.3.refs_4_), channel_id=1, source_target_pairs={{16,20},{17,21},{18,22},{19,23},{20,16},{21,17},{22,18},{23,19},{2... | collective-permute-start | bytes 811016 | tf_op jit(solution)/shard_map/ppermute | solution.py:134
  55.5 1.9 %collective-permute-start.6 = (bf16[528,256]{1,0:T(8,128)(2,1)}, bf16[528,256]{1,0:T(8,128)(2,1)S(1)}, u32[]{:S(2)}, u32[]{:S(2)}) collective-permute-start(bf16[528,256]{1,0:T(8,128)(2,1)} %collective-permute-done.4.refs_5_), channel_id=1, source_target_pairs={{16,20},{17,21},{18,22},{19,23},{20,16},{21,17},{22,18},{23,19},{2... | collective-permute-start | bytes 811016 | tf_op jit(solution)/shard_map/ppermute | solution.py:134
  57.6 5.8 %collective-permute-done.5.refs_6_ = bf16[528,256]{1,0:T(8,128)(2,1)S(1)} collective-permute-done((bf16[528,256]{1,0:T(8,128)(2,1)}, bf16[528,256]{1,0:T(8,128)(2,1)S(1)}, u32[]{:S(2)}, u32[]{:S(2)}) %collective-permute-start.5) | collective-permute-done | bytes 270368 | tf_op jit(solution)/shard_map/ppermute | solution.py:134
  64.1 2.9 %collective-permute-start.11 = (bf16[256,512]{1,0:T(8,128)(2,1)S(1)}, bf16[256,512]{1,0:T(8,128)(2,1)}, u32[]{:S(2)}, u32[]{:S(2)}) collective-permute-start(bf16[256,512]{1,0:T(8,128)(2,1)S(1)} %copy-done.2), channel_id=1, source_target_pairs={{0,16},{1,17},{2,18},{3,19},{4,20},{5,21},{6,22},{7,23},{8,24},{9,... | collective-permute-start | bytes 786440 | tf_op jit(solution)/shard_map/ppermute | solution.py:134
  68.8 1.7 %collective-permute-start.9 = (bf16[256,768]{1,0:T(8,128)(2,1)S(1)}, bf16[256,768]{1,0:T(8,128)(2,1)S(1)}, u32[]{:S(2)}, u32[]{:S(2)}) collective-permute-start(bf16[256,768]{1,0:T(8,128)(2,1)S(1)} %window_heads.1.l0), channel_id=1, source_target_pairs={{0,4},{1,5},{2,6},{3,7},{4,0},{5,1},{6,2},{7,3},{8,12},{9,13},{10,... | collective-permute-start | bytes 1179656 | tf_op jit(solution)/shard_map/ppermute | solution.py:134
  71.0 6.1 %routed_near.1 = (f32[4,256,256]{2,1,0:T(8,128)S(1)}, f32[4,256,128]{2,1,0:T(8,128)S(1)}) custom-call(s32[16]{0:T(128)S(1)} %mul.8.shift, bf16[784,256]{1,0:T(8,128)(2,1)S(1)} %fusion.1.refs_0_, bf16[784,256]{1,0:T(8,128)(2,1)S(1)} %collective-permute-done.refs_1_, bf16[784,256]{1,0:T(8,128)(2,1)} %collective-permute-done.1.refs_2_, ...), custom_call_target="tpu_custom_call" | custom-call | tf_op jit(solution)/shard_map/routed_near/pallas_call | solution.py:261
  77.2 6.1 %routed_past.1.routed = bf16[4,256,256]{2,1,0:T(8,128)(2,1)S(1)} custom-call(s32[1]{0:T(128)} %bitcast.half, bf16[784,256]{1,0:T(8,128)(2,1)S(1)} %fusion.1.refs_0_, bf16[784,256]{1,0:T(8,128)(2,1)S(1)} %collective-permute-done.refs_1_, bf16[784,256]{1,0:T(8,128)(2,1)} %collective-permute-done.1.refs_2_, bf16[784,256]{1,0:T(8,128)(2,1)} %collective-permute-done.2.refs_3_, ...), custom_call_target="tpu_custom_call" | custom-call | tf_op jit(solution)/shard_map/routed_past/pallas_call | solution.py:280
  84.8 5.4 %collective-permute-done.11.wr1 = bf16[256,512]{1,0:T(8,128)(2,1)} collective-permute-done((bf16[256,512]{1,0:T(8,128)(2,1)S(1)}, bf16[256,512]{1,0:T(8,128)(2,1)}, u32[]{:S(2)}, u32[]{:S(2)}) %collective-permute-start.11) | collective-permute-done | bytes 262176 | tf_op jit(solution)/shard_map/ppermute | solution.py:134
  90.3 3.5 %project.3 = (bf16[256,1024]{1,0:T(8,128)(2,1)S(1)}, bf16[256,1024]{1,0:T(8,128)(2,1)}) custom-call(s32[4]{0:T(128)S(1)} %get-tuple-element.23.use, bf16[4,256,256]{2,1,0:T(8,128)(2,1)S(1)} %routed_past.1.routed, bf16[256,768]{1,0:T(8,128)(2,1)S(1)} %window_heads.1.l0, bf16[256,768]{1,0:T(8,128)(2,1)S(1)} %collective-permute-done.8.l1, ...), custom_call_target="tpu_custom_call" | custom-call | tf_op jit(solution)/shard_map/project/pallas_call | solution.py:323
  94.5 3.4 %project.2 = (bf16[256,1024]{1,0:T(8,128)(2,1)S(1)}, bf16[256,1024]{1,0:T(8,128)(2,1)}) custom-call(s32[4]{0:T(128)S(1)} %get-tuple-element.22.use, bf16[4,256,256]{2,1,0:T(8,128)(2,1)S(1)} %routed_past.1.routed, bf16[256,768]{1,0:T(8,128)(2,1)S(1)} %window_heads.1.l0, bf16[256,768]{1,0:T(8,128)(2,1)S(1)} %collective-permute-done.8.l1, ...), custom_call_target="tpu_custom_call" | custom-call | tf_op jit(solution)/shard_map/project/pallas_call | solution.py:323
  101.6 1.6 %collective-permute-start.16 = (bf16[256,512]{1,0:T(8,128)(2,1)S(1)}, bf16[256,512]{1,0:T(8,128)(2,1)S(1)}, u32[]{:S(2)}, u32[]{:S(2)}) collective-permute-start(bf16[256,512]{1,0:T(8,128)(2,1)S(1)} %select_convert_fusion.1), channel_id=1, source_target_pairs={{0,2},{1,3},{2,0},{3,1},{4,6},{5,7},{6,4},{7,5},{8,10},{9,11},{10,... | collective-permute-start | bytes 786440 | tf_op jit(solution)/shard_map/ppermute | solution.py:134
  103.2 6.8 %collective-permute-done.19 = bf16[256,512]{1,0:T(8,128)(2,1)S(1)} collective-permute-done((bf16[256,512]{1,0:T(8,128)(2,1)S(1)}, bf16[256,512]{1,0:T(8,128)(2,1)S(1)}, u32[]{:S(2)}, u32[]{:S(2)}) %collective-permute-start.19) | collective-permute-done | bytes 262176 | tf_op jit(solution)/shard_map/ppermute | solution.py:134
  110.2 1.9 %collective-permute-start.20 = (bf16[256,512]{1,0:T(8,128)(2,1)S(1)}, bf16[256,512]{1,0:T(8,128)(2,1)S(1)}, u32[]{:S(2)}, u32[]{:S(2)}) collective-permute-start(bf16[256,512]{1,0:T(8,128)(2,1)S(1)} %add_convert_fusion), channel_id=1, source_target_pairs={{0,8},{1,12},{2,10},{3,14},{4,0},{5,4},{6,2},{7,6},{8,1},{9,5},{10... | collective-permute-start | bytes 786440 | tf_op jit(solution)/shard_map/ppermute | solution.py:134
  112.1 2.6 %collective-permute-done.16 = bf16[256,512]{1,0:T(8,128)(2,1)S(1)} collective-permute-done((bf16[256,512]{1,0:T(8,128)(2,1)S(1)}, bf16[256,512]{1,0:T(8,128)(2,1)S(1)}, u32[]{:S(2)}, u32[]{:S(2)}) %collective-permute-start.16) | collective-permute-done | bytes 262176 | tf_op jit(solution)/shard_map/ppermute | solution.py:134
  114.8 1.9 %collective-permute-start.17 = (bf16[256,512]{1,0:T(8,128)(2,1)S(1)}, bf16[256,512]{1,0:T(8,128)(2,1)S(1)}, u32[]{:S(2)}, u32[]{:S(2)}) collective-permute-start(bf16[256,512]{1,0:T(8,128)(2,1)S(1)} %add_convert_fusion.1), channel_id=1, source_target_pairs={{0,0},{1,4},{2,2},{3,6},{4,8},{5,12},{6,10},{7,14},{8,9},{9,13},{1... | collective-permute-start | bytes 786440 | tf_op jit(solution)/shard_map/ppermute | solution.py:134
  116.8 3.6 %collective-permute-done.20 = bf16[256,512]{1,0:T(8,128)(2,1)S(1)} collective-permute-done((bf16[256,512]{1,0:T(8,128)(2,1)S(1)}, bf16[256,512]{1,0:T(8,128)(2,1)S(1)}, u32[]{:S(2)}, u32[]{:S(2)}) %collective-permute-start.20) | collective-permute-done | bytes 262176 | tf_op jit(solution)/shard_map/ppermute | solution.py:134
  120.4 6.4 %collective-permute-done.17 = bf16[256,512]{1,0:T(8,128)(2,1)S(1)} collective-permute-done((bf16[256,512]{1,0:T(8,128)(2,1)S(1)}, bf16[256,512]{1,0:T(8,128)(2,1)S(1)}, u32[]{:S(2)}, u32[]{:S(2)}) %collective-permute-start.17) | collective-permute-done | bytes 262176 | tf_op jit(solution)/shard_map/ppermute | solution.py:134
  (71 shorter events, 13.2 us)
Async XLA Ops:
  2.2 37.4 %collective-permute-start.7 = (bf16[2,256,768]{2,1,0:T(8,128)(2,1)}, bf16[2,256,768]{2,1,0:T(8,128)(2,1)}, u32[]{:S(2)}, u32[]{:S(2)}) collective-permute-start(bf16[2,256,768]{2,1,0:T(8,128)(2,1)} %slice.32), channel_id=1, source_target_pairs={{0,4},{1,5},{2,6},{3,7},{4,8},{5,9},{6,10},{7,11},{8,12},{9,13},{1... | collective-permute-start | bytes 2359304 | tf_op jit(solution)/shard_map/ppermute | solution.py:134
  5.7 33.9 %copy-start.1 = (bf16[3,256,768]{2,1,0:T(8,128)(2,1)S(1)}, bf16[3,256,768]{2,1,0:T(8,128)(2,1)}, u32[]{:S(2)}) copy-start(bf16[3,256,768]{2,1,0:T(8,128)(2,1)} %qkv.1) | copy-start | bytes 3538948
  5.7 16.8 %collective-permute-start.3 = (bf16[528,256]{1,0:T(8,128)(2,1)S(1)}, bf16[528,256]{1,0:T(8,128)(2,1)}, u32[]{:S(2)}, u32[]{:S(2)}) collective-permute-start(bf16[528,256]{1,0:T(8,128)(2,1)S(1)} %slice.40), channel_id=1, source_target_pairs={{0,16},{1,17},{2,18},{3,19},{4,20},{5,21},{6,22},{7,23},{8,24},{9,... | collective-permute-start | bytes 811016 | tf_op jit(solution)/shard_map/ppermute | solution.py:134
  7.2 32.4 %collective-permute-start = (bf16[784,256]{1,0:T(8,128)(2,1)S(1)}, bf16[784,256]{1,0:T(8,128)(2,1)S(1)}, u32[]{:S(2)}, u32[]{:S(2)}) collective-permute-start(bf16[784,256]{1,0:T(8,128)(2,1)S(1)} %fusion.1.refs_0_), channel_id=1, source_target_pairs={{0,8},{1,9},{2,10},{3,11},{4,12},{5,13},{6,14},{7,15},{8,0},{9,1},... | collective-permute-start | bytes 1204232 | tf_op jit(solution)/shard_map/ppermute | solution.py:134
  22.5 33.1 %collective-permute-start.4 = (bf16[528,256]{1,0:T(8,128)(2,1)}, bf16[528,256]{1,0:T(8,128)(2,1)}, u32[]{:S(2)}, u32[]{:S(2)}) collective-permute-start(bf16[528,256]{1,0:T(8,128)(2,1)} %collective-permute-done.3.refs_4_), channel_id=1, source_target_pairs={{16,24},{17,25},{18,26},{19,27},{20,28},{21,29},{22,30},{23,31},{2... | collective-permute-start | bytes 811016 | tf_op jit(solution)/shard_map/ppermute | solution.py:134
  25.3 19.6 %collective-permute-start.12 = (bf16[256,512]{1,0:T(8,128)(2,1)}, bf16[256,512]{1,0:T(8,128)(2,1)}, u32[]{:S(2)}, u32[]{:S(2)}) collective-permute-start(bf16[256,512]{1,0:T(8,128)(2,1)} %get-tuple-element.19), channel_id=1, source_target_pairs={{0,16},{1,17},{2,18},{3,19},{4,20},{5,21},{6,22},{7,23},{8,24},{9,... | collective-permute-start | bytes 786440 | tf_op jit(solution)/shard_map/ppermute | solution.py:134
  25.3 32.2 %collective-permute-start.1 = (bf16[784,256]{1,0:T(8,128)(2,1)S(1)}, bf16[784,256]{1,0:T(8,128)(2,1)}, u32[]{:S(2)}, u32[]{:S(2)}) collective-permute-start(bf16[784,256]{1,0:T(8,128)(2,1)S(1)} %fusion.1.refs_0_), channel_id=1, source_target_pairs={{0,4},{1,5},{2,6},{3,7},{4,0},{5,1},{6,2},{7,3},{8,12},{9,13},{10,... | collective-permute-start | bytes 1204232 | tf_op jit(solution)/shard_map/ppermute | solution.py:134
  39.5 24.6 %collective-permute-start.2 = (bf16[784,256]{1,0:T(8,128)(2,1)S(1)}, bf16[784,256]{1,0:T(8,128)(2,1)}, u32[]{:S(2)}, u32[]{:S(2)}) collective-permute-start(bf16[784,256]{1,0:T(8,128)(2,1)S(1)} %collective-permute-done.refs_1_), channel_id=1, source_target_pairs={{0,4},{1,5},{2,6},{3,7},{4,0},{5,1},{6,2},{7,3},{8,12},{9,13},{10,... | collective-permute-start | bytes 1204232 | tf_op jit(solution)/shard_map/ppermute | solution.py:134
  39.6 31.4 %copy-start.12 = (s32[4]{0:T(128)S(1)}, s32[4]{0:T(128)}, u32[]{:S(2)}) copy-start(s32[4]{0:T(128)} %constant.112) | copy-start | bytes 52
  39.6 31.4 %copy-start.13 = (s32[4]{0:T(128)S(1)}, s32[4]{0:T(128)}, u32[]{:S(2)}) copy-start(s32[4]{0:T(128)} %constant.116) | copy-start | bytes 52
  42.8 27.7 %collective-permute-start.8 = (bf16[256,768]{1,0:T(8,128)(2,1)S(1)}, bf16[256,768]{1,0:T(8,128)(2,1)S(1)}, u32[]{:S(2)}, u32[]{:S(2)}) collective-permute-start(bf16[256,768]{1,0:T(8,128)(2,1)S(1)} %window_heads.1.l0), channel_id=1, source_target_pairs={{0,8},{1,9},{2,10},{3,11},{4,12},{5,13},{6,14},{7,15},{8,0},{9,1},... | collective-permute-start | bytes 1179656 | tf_op jit(solution)/shard_map/ppermute | solution.py:134
  44.9 18.5 %collective-permute-start.5 = (bf16[528,256]{1,0:T(8,128)(2,1)}, bf16[528,256]{1,0:T(8,128)(2,1)S(1)}, u32[]{:S(2)}, u32[]{:S(2)}) collective-permute-start(bf16[528,256]{1,0:T(8,128)(2,1)} %collective-permute-done.3.refs_4_), channel_id=1, source_target_pairs={{16,20},{17,21},{18,22},{19,23},{20,16},{21,17},{22,18},{23,19},{2... | collective-permute-start | bytes 811016 | tf_op jit(solution)/shard_map/ppermute | solution.py:134
  55.5 12.5 %collective-permute-start.6 = (bf16[528,256]{1,0:T(8,128)(2,1)}, bf16[528,256]{1,0:T(8,128)(2,1)S(1)}, u32[]{:S(2)}, u32[]{:S(2)}) collective-permute-start(bf16[528,256]{1,0:T(8,128)(2,1)} %collective-permute-done.4.refs_5_), channel_id=1, source_target_pairs={{16,20},{17,21},{18,22},{19,23},{20,16},{21,17},{22,18},{23,19},{2... | collective-permute-start | bytes 811016 | tf_op jit(solution)/shard_map/ppermute | solution.py:134
  57.5 25.8 %collective-permute-start.13 = (bf16[256,512]{1,0:T(8,128)(2,1)}, bf16[256,512]{1,0:T(8,128)(2,1)}, u32[]{:S(2)}, u32[]{:S(2)}) collective-permute-start(bf16[256,512]{1,0:T(8,128)(2,1)} %get-tuple-element.18), channel_id=1, source_target_pairs={{0,16},{1,17},{2,18},{3,19},{4,20},{5,21},{6,22},{7,23},{8,24},{9,... | collective-permute-start | bytes 786440 | tf_op jit(solution)/shard_map/ppermute | solution.py:134
  64.1 20.7 %collective-permute-start.14 = (bf16[256,512]{1,0:T(8,128)(2,1)}, bf16[256,512]{1,0:T(8,128)(2,1)}, u32[]{:S(2)}, u32[]{:S(2)}) collective-permute-start(bf16[256,512]{1,0:T(8,128)(2,1)} %get-tuple-element.17), channel_id=1, source_target_pairs={{0,16},{1,17},{2,18},{3,19},{4,20},{5,21},{6,22},{7,23},{8,24},{9,... | collective-permute-start | bytes 786440 | tf_op jit(solution)/shard_map/ppermute | solution.py:134
  64.1 26.2 %collective-permute-start.11 = (bf16[256,512]{1,0:T(8,128)(2,1)S(1)}, bf16[256,512]{1,0:T(8,128)(2,1)}, u32[]{:S(2)}, u32[]{:S(2)}) collective-permute-start(bf16[256,512]{1,0:T(8,128)(2,1)S(1)} %copy-done.2), channel_id=1, source_target_pairs={{0,16},{1,17},{2,18},{3,19},{4,20},{5,21},{6,22},{7,23},{8,24},{9,... | collective-permute-start | bytes 786440 | tf_op jit(solution)/shard_map/ppermute | solution.py:134
  68.8 21.5 %collective-permute-start.9 = (bf16[256,768]{1,0:T(8,128)(2,1)S(1)}, bf16[256,768]{1,0:T(8,128)(2,1)S(1)}, u32[]{:S(2)}, u32[]{:S(2)}) collective-permute-start(bf16[256,768]{1,0:T(8,128)(2,1)S(1)} %window_heads.1.l0), channel_id=1, source_target_pairs={{0,4},{1,5},{2,6},{3,7},{4,0},{5,1},{6,2},{7,3},{8,12},{9,13},{10,... | collective-permute-start | bytes 1179656 | tf_op jit(solution)/shard_map/ppermute | solution.py:134
  70.5 19.7 %collective-permute-start.10 = (bf16[256,768]{1,0:T(8,128)(2,1)S(1)}, bf16[256,768]{1,0:T(8,128)(2,1)S(1)}, u32[]{:S(2)}, u32[]{:S(2)}) collective-permute-start(bf16[256,768]{1,0:T(8,128)(2,1)S(1)} %collective-permute-done.8.l1), channel_id=1, source_target_pairs={{0,4},{1,5},{2,6},{3,7},{4,0},{5,1},{6,2},{7,3},{8,12},{9,13},{10,... | collective-permute-start | bytes 1179656 | tf_op jit(solution)/shard_map/ppermute | solution.py:134
  94.5 4.8 %collective-permute-start.18 = (bf16[256,1024]{1,0:T(8,128)(2,1)}, bf16[256,1024]{1,0:T(8,128)(2,1)}, u32[]{:S(2)}, u32[]{:S(2)}) collective-permute-start(bf16[256,1024]{1,0:T(8,128)(2,1)} %get-tuple-element.16), channel_id=1, source_target_pairs={{0,1},{1,0},{2,3},{3,2},{4,5},{5,4},{6,7},{7,6},{8,9},{9,8},{10,11... | collective-permute-start | bytes 1572872 | tf_op jit(solution)/shard_map/ppermute | solution.py:134
  98.8 2.6 %collective-permute-start.15 = (bf16[256,1024]{1,0:T(8,128)(2,1)}, bf16[256,1024]{1,0:T(8,128)(2,1)S(1)}, u32[]{:S(2)}, u32[]{:S(2)}) collective-permute-start(bf16[256,1024]{1,0:T(8,128)(2,1)} %get-tuple-element.14), channel_id=1, source_target_pairs={{0,1},{1,0},{2,3},{3,2},{4,5},{5,4},{6,7},{7,6},{8,9},{9,8},{10,11... | collective-permute-start | bytes 1572872 | tf_op jit(solution)/shard_map/ppermute | solution.py:134
  100.8 9.2 %collective-permute-start.19 = (bf16[256,512]{1,0:T(8,128)(2,1)S(1)}, bf16[256,512]{1,0:T(8,128)(2,1)S(1)}, u32[]{:S(2)}, u32[]{:S(2)}) collective-permute-start(bf16[256,512]{1,0:T(8,128)(2,1)S(1)} %select_convert_fusion), channel_id=1, source_target_pairs={{0,2},{1,3},{2,0},{3,1},{4,6},{5,7},{6,4},{7,5},{8,10},{9,11},{10,... | collective-permute-start | bytes 786440 | tf_op jit(solution)/shard_map/ppermute | solution.py:134
  101.6 13.1 %collective-permute-start.16 = (bf16[256,512]{1,0:T(8,128)(2,1)S(1)}, bf16[256,512]{1,0:T(8,128)(2,1)S(1)}, u32[]{:S(2)}, u32[]{:S(2)}) collective-permute-start(bf16[256,512]{1,0:T(8,128)(2,1)S(1)} %select_convert_fusion.1), channel_id=1, source_target_pairs={{0,2},{1,3},{2,0},{3,1},{4,6},{5,7},{6,4},{7,5},{8,10},{9,11},{10,... | collective-permute-start | bytes 786440 | tf_op jit(solution)/shard_map/ppermute | solution.py:134
  110.2 10.2 %collective-permute-start.20 = (bf16[256,512]{1,0:T(8,128)(2,1)S(1)}, bf16[256,512]{1,0:T(8,128)(2,1)S(1)}, u32[]{:S(2)}, u32[]{:S(2)}) collective-permute-start(bf16[256,512]{1,0:T(8,128)(2,1)S(1)} %add_convert_fusion), channel_id=1, source_target_pairs={{0,8},{1,12},{2,10},{3,14},{4,0},{5,4},{6,2},{7,6},{8,1},{9,5},{10... | collective-permute-start | bytes 786440 | tf_op jit(solution)/shard_map/ppermute | solution.py:134
  114.8 12.0 %collective-permute-start.17 = (bf16[256,512]{1,0:T(8,128)(2,1)S(1)}, bf16[256,512]{1,0:T(8,128)(2,1)S(1)}, u32[]{:S(2)}, u32[]{:S(2)}) collective-permute-start(bf16[256,512]{1,0:T(8,128)(2,1)S(1)} %add_convert_fusion.1), channel_id=1, source_target_pairs={{0,0},{1,4},{2,2},{3,6},{4,8},{5,12},{6,10},{7,14},{8,9},{9,13},{1... | collective-permute-start | bytes 786440 | tf_op jit(solution)/shard_map/ppermute | solution.py:134
  (12 other events, 95.4 us)
where the time goes:
time: 128 us
  waiting for transfers between devices  48.1 us (38%)
  starting transfers between devices  47.7 us (37%)
  Pallas kernels  22.3 us (17%)
  local copies, waits for them, and re-layouts  6.24 us (5%)
  other arithmetic  3.02 us (2%)
    ppermute x21, waiting for transfers between devices, moved(): return lax.ppermute(block, AXES, route)  48.1 us
    ppermute x21, starting transfers between devices, moved(): return lax.ppermute(block, AXES, route)  47.7 us
    pallas_call x2, Pallas kernels, project(): pl.pallas_call(project_body, in_specs=[SCALARS] + [WHOLE] * (5 + len(weig...  6.9 us
    pallas_call x1, Pallas kernels, routed_past(): pl.pallas_call(past_body, in_specs=[SCALARS] + [WHOLE] * 10, out_specs=WH...  6.12 us
    pallas_call x1, Pallas kernels, routed_near(): pl.pallas_call(near_body, in_specs=[SCALARS] + [WHOLE] * 4, out_specs=(WH...  6.11 us
    pallas_call x1, Pallas kernels, window_heads(): pl.pallas_call(window_body, in_specs=[SCALARS] + [WHOLE] * 2, out_specs=W...  3.16 us
    unnamed x31, local copies, waits for them, and re-layouts  3.08 us
  transfers between devices with their start and end apart: 21, of which 9 were waited for; matrix products, arithmetic and copies ran while one was open for 2% of the time, Pallas kernels for 15%

commit v1 on v0

--- a/solution.py
+++ b/solution.py
@@ -289,6 +289,67 @@
         compiler_params=pltpu.CompilerParams(vmem_limit_bytes=20 << 20),
         name="routed_past",
     )(half.astype(jnp.int32).reshape(1), *near, *past, acc, stat)
+
+
+def combine_body(here, keep, got, stay, cross):
+    width = stay.shape[1]
+    own, other = slice(0, width), slice(width, 2 * width)
+
+    def add(at, out):
+        total = keep[:, at].astype(jnp.float32) + got[:, at].astype(jnp.float32)
+        out[...] = total.astype(out.dtype)
+
+    @pl.when(here[0] == 1)
+    def _():
+        add(own, stay)
+        add(other, cross)
+
+    @pl.when(here[0] == 0)
+    def _():
+        add(other, stay)
+        add(own, cross)
+
+
+def combine(here, keep, got):
+    shape = jax.ShapeDtypeStruct((keep.shape[0], keep.shape[1] // 2), keep.dtype)
+    return pl.pallas_call(
+        combine_body,
+        in_specs=[SCALARS, WHOLE, WHOLE],
+        out_specs=(WHOLE, WHOLE),
+        out_shape=(shape, shape),
+        compiler_params=pltpu.CompilerParams(vmem_limit_bytes=6 << 20),
+        name="combine",
+    )(here, keep, got)
+
+
+def finish_body(ahead, s0, c0, s1, c1, out):
+    width = s0.shape[1]
+
+    def add(stay, cross, at):
+        total = stay[...].astype(jnp.float32) + cross[...].astype(jnp.float32)
+        out[:, at : at + width] = total.astype(out.dtype)
+
+    @pl.when(ahead[0] == 1)
+    def _():
+        add(s0, c0, 0)
+        add(s1, c1, width)
+
+    @pl.when(ahead[0] == 0)
+    def _():
+        add(s0, c0, width)
+        add(s1, c1, 0)
+
+
+def finish(ahead, pieces):
+    rows, width = pieces[0].shape
+    return pl.pallas_call(
+        finish_body,
+        in_specs=[SCALARS] + [WHOLE] * 4,
+        out_specs=WHOLE,
+        out_shape=jax.ShapeDtypeStruct((rows, 2 * width), jnp.bfloat16),
+        compiler_params=pltpu.CompilerParams(vmem_limit_bytes=6 << 20),
+        name="finish",
+    )(ahead, *pieces)
 
 
 def project_body(use, routed, l0, l1, l2, l3, wr0, wl0, wr1, *rest):
@@ -374,30 +435,24 @@
     slots = jnp.array([0, 2, 1, 3], jnp.int32)
     kept = jnp.where(slots % 2 == low ^ core, 1, 2)
     weights = (wo_routed, wo_local, other_routed, *others)
-    here = half == far
-
-    def target(flip):
+    here = (half == far).astype(jnp.int32).reshape(1)
+
+    def target(flip, turn):
         def to(s, h):
             r, z, y = split_seq(s)
-            return r * 4 + (z ^ y ^ flip) * 2 + h % 2, (h // 2) * 2 + z
+            return r * 4 + (z ^ y ^ flip) * 2 + h % 2, ((h // 2) ^ turn) * 2 + z
 
         return to
 
-    done = []
+    pieces = []
     for flip in range(2):
         use = jnp.where(slots // 2 == low ^ flip, kept, 0).astype(jnp.int32)
         keep, send = project(use, routed, local, weights)
         got = moved(send, lambda s, h: (s, h ^ 1))
-        both = keep.astype(jnp.float32) + got.astype(jnp.float32)
-        width = both.shape[1] // 2
-        mine = jnp.where(here, both[:, :width], both[:, width:])
-        theirs = jnp.where(here, both[:, width:], both[:, :width]).astype(jnp.bfloat16)
-        total = mine + moved(theirs, lambda s, h: (s, h ^ 2)).astype(jnp.float32)
-        done.append(moved(total.astype(jnp.bfloat16), target(flip)))
-    ahead = mid == core
-    return jnp.concatenate(
-        [jnp.where(ahead, done[0], done[1]), jnp.where(ahead, done[1], done[0])], axis=1
-    )
+        stay, cross = combine(here, keep, got)
+        cross = moved(cross, target(flip, 1))
+        pieces += [moved(stay, target(flip, 0)), cross]
+    return finish((mid == core).astype(jnp.int32).reshape(1), pieces)
 
 
 def on_device(*arrays):

time: 128 us -> 125 us (0.977)
  the two profiles are of different devices: /device:TPU:26 before, /device:TPU:8 now
where the time goes in v1:
time: 125 us; the launch traced here: 124 us
  starting transfers between devices  56.6 us (45%)
  waiting for transfers between devices  39.6 us (32%)
  Pallas kernels  20.2 us (16%)
  local copies, waits for them, and re-layouts  7.29 us (6%)
    ppermute x21, starting transfers between devices, moved(): return lax.ppermute(block, AXES, route)  56.6 us
    ppermute x21, waiting for transfers between devices, moved(): return lax.ppermute(block, AXES, route)  39.6 us
    pallas_call x2, Pallas kernels, project(): pl.pallas_call(project_body, in_specs=[SCALARS] + [WHOLE] * (5 + len(weig...  6.91 us
    pallas_call x1, Pallas kernels, routed_near(): pl.pallas_call(near_body, in_specs=[SCALARS] + [WHOLE] * 4, out_specs=(WH...  6.12 us
    unnamed x33, local copies, waits for them, and re-layouts  4.11 us
    pallas_call x1, Pallas kernels, window_heads(): pl.pallas_call(window_body, in_specs=[SCALARS] + [WHOLE] * 2, out_specs=W...  3.16 us
  transfers between devices with their start and end apart: 21, of which 9 were waited for; matrix products, arithmetic and copies ran while one was open for 1% of the time, Pallas kernels for 13%

profile of v1, /device:TPU:8, one launch (start us, length us, event | category | flops | bytes accessed | tf_op | source)
XLA Modules:
  0.0 124.1 jit_solution(5352326468151209274)
XLA Ops:
  0.0 2.2 %slice.16 = bf16[2,256,768]{2,1,0:T(8,128)(2,1)} slice(bf16[3,256,768]{2,1,0:T(8,128)(2,1)} %qkv.1), slice={[1:3], [0:256], [0:768]} | slice | bytes 1572864 | tf_op jit(solution)/shard_map/slice | solution.py:408
  2.2 3.4 %collective-permute-start.7 = (bf16[2,256,768]{2,1,0:T(8,128)(2,1)}, bf16[2,256,768]{2,1,0:T(8,128)(2,1)}, u32[]{:S(2)}, u32[]{:S(2)}) collective-permute-start(bf16[2,256,768]{2,1,0:T(8,128)(2,1)} %slice.16), channel_id=1, source_target_pairs={{0,4},{1,5},{2,6},{3,7},{4,8},{5,9},{6,10},{7,11},{8,12},{9,13},{1... | collective-permute-start | bytes 2359304 | tf_op jit(solution)/shard_map/ppermute | solution.py:134
  5.7 5.3 %collective-permute-start.3 = (bf16[528,256]{1,0:T(8,128)(2,1)S(1)}, bf16[528,256]{1,0:T(8,128)(2,1)}, u32[]{:S(2)}, u32[]{:S(2)}) collective-permute-start(bf16[528,256]{1,0:T(8,128)(2,1)S(1)} %slice.20), channel_id=1, source_target_pairs={{0,16},{1,17},{2,18},{3,19},{4,20},{5,21},{6,22},{7,23},{8,24},{9,... | collective-permute-start | bytes 811016 | tf_op jit(solution)/shard_map/ppermute | solution.py:134
  11.5 10.0 %collective-permute-done.3.refs_4_ = bf16[528,256]{1,0:T(8,128)(2,1)} collective-permute-done((bf16[528,256]{1,0:T(8,128)(2,1)S(1)}, bf16[528,256]{1,0:T(8,128)(2,1)}, u32[]{:S(2)}, u32[]{:S(2)}) %collective-permute-start.3) | collective-permute-done | bytes 270368 | tf_op jit(solution)/shard_map/ppermute | solution.py:134
  23.8 4.1 %collective-permute-start.12 = (bf16[256,512]{1,0:T(8,128)(2,1)}, bf16[256,512]{1,0:T(8,128)(2,1)}, u32[]{:S(2)}, u32[]{:S(2)}) collective-permute-start(bf16[256,512]{1,0:T(8,128)(2,1)} %get-tuple-element.27), channel_id=1, source_target_pairs={{0,16},{1,17},{2,18},{3,19},{4,20},{5,21},{6,22},{7,23},{8,24},{9,... | collective-permute-start | bytes 786440 | tf_op jit(solution)/shard_map/ppermute | solution.py:134
  27.9 14.2 %collective-permute-start.1 = (bf16[784,256]{1,0:T(8,128)(2,1)S(1)}, bf16[784,256]{1,0:T(8,128)(2,1)}, u32[]{:S(2)}, u32[]{:S(2)}) collective-permute-start(bf16[784,256]{1,0:T(8,128)(2,1)S(1)} %fusion.1.refs_0_), channel_id=1, source_target_pairs={{0,4},{1,5},{2,6},{3,7},{4,0},{5,1},{6,2},{7,3},{8,12},{9,13},{10,... | collective-permute-start | bytes 1204232 | tf_op jit(solution)/shard_map/ppermute | solution.py:134
  42.2 3.2 %window_heads.1.l0 = bf16[256,768]{1,0:T(8,128)(2,1)S(1)} custom-call(s32[1]{0:T(128)} %bitcast.5.first, bf16[3,256,768]{2,1,0:T(8,128)(2,1)S(1)} %copy-done.1, bf16[2,256,768]{2,1,0:T(8,128)(2,1)} %collective-permute-done.7.tail), custom_call_target="tpu_custom_call" | custom-call | tf_op jit(solution)/shard_map/window_heads/pallas_call | solution.py:171
  45.4 2.1 %collective-permute-start.8 = (bf16[256,768]{1,0:T(8,128)(2,1)S(1)}, bf16[256,768]{1,0:T(8,128)(2,1)S(1)}, u32[]{:S(2)}, u32[]{:S(2)}) collective-permute-start(bf16[256,768]{1,0:T(8,128)(2,1)S(1)} %window_heads.1.l0), channel_id=1, source_target_pairs={{0,8},{1,9},{2,10},{3,11},{4,12},{5,13},{6,14},{7,15},{8,0},{9,1},... | collective-permute-start | bytes 1179656 | tf_op jit(solution)/shard_map/ppermute | solution.py:134
  48.8 3.5 %collective-permute-done.1.refs_2_ = bf16[784,256]{1,0:T(8,128)(2,1)} collective-permute-done((bf16[784,256]{1,0:T(8,128)(2,1)S(1)}, bf16[784,256]{1,0:T(8,128)(2,1)}, u32[]{:S(2)}, u32[]{:S(2)}) %collective-permute-start.1) | collective-permute-done | bytes 401440 | tf_op jit(solution)/shard_map/ppermute | solution.py:134
  52.4 7.8 %collective-permute-start.13 = (bf16[256,512]{1,0:T(8,128)(2,1)}, bf16[256,512]{1,0:T(8,128)(2,1)}, u32[]{:S(2)}, u32[]{:S(2)}) collective-permute-start(bf16[256,512]{1,0:T(8,128)(2,1)} %get-tuple-element.26), channel_id=1, source_target_pairs={{0,16},{1,17},{2,18},{3,19},{4,20},{5,21},{6,22},{7,23},{8,24},{9,... | collective-permute-start | bytes 786440 | tf_op jit(solution)/shard_map/ppermute | solution.py:134
  60.9 5.8 %collective-permute-start.14 = (bf16[256,512]{1,0:T(8,128)(2,1)}, bf16[256,512]{1,0:T(8,128)(2,1)}, u32[]{:S(2)}, u32[]{:S(2)}) collective-permute-start(bf16[256,512]{1,0:T(8,128)(2,1)} %get-tuple-element.25), channel_id=1, source_target_pairs={{0,16},{1,17},{2,18},{3,19},{4,20},{5,21},{6,22},{7,23},{8,24},{9,... | collective-permute-start | bytes 786440 | tf_op jit(solution)/shard_map/ppermute | solution.py:134
  67.5 1.8 %collective-permute-start.9 = (bf16[256,768]{1,0:T(8,128)(2,1)S(1)}, bf16[256,768]{1,0:T(8,128)(2,1)S(1)}, u32[]{:S(2)}, u32[]{:S(2)}) collective-permute-start(bf16[256,768]{1,0:T(8,128)(2,1)S(1)} %window_heads.1.l0), channel_id=1, source_target_pairs={{0,4},{1,5},{2,6},{3,7},{4,0},{5,1},{6,2},{7,3},{8,12},{9,13},{10,... | collective-permute-start | bytes 1179656 | tf_op jit(solution)/shard_map/ppermute | solution.py:134
  69.7 6.1 %routed_near.1 = (f32[4,256,256]{2,1,0:T(8,128)S(1)}, f32[4,256,128]{2,1,0:T(8,128)S(1)}) custom-call(s32[16]{0:T(128)S(1)} %mul.8.shift, bf16[784,256]{1,0:T(8,128)(2,1)S(1)} %fusion.1.refs_0_, bf16[784,256]{1,0:T(8,128)(2,1)S(1)} %collective-permute-done.refs_1_, bf16[784,256]{1,0:T(8,128)(2,1)} %collective-permute-done.1.refs_2_, ...), custom_call_target="tpu_custom_call" | custom-call | tf_op jit(solution)/shard_map/routed_near/pallas_call | solution.py:261
  75.8 1.8 %routed_past.1.routed = bf16[4,256,256]{2,1,0:T(8,128)(2,1)S(1)} custom-call(s32[1]{0:T(128)} %bitcast.2.half, bf16[784,256]{1,0:T(8,128)(2,1)S(1)} %fusion.1.refs_0_, bf16[784,256]{1,0:T(8,128)(2,1)S(1)} %collective-permute-done.refs_1_, bf16[784,256]{1,0:T(8,128)(2,1)} %collective-permute-done.1.refs_2_, bf16[784,256]{1,0:T(8,128)(2,1)} %collective-permute-done.2.refs_3_, ...), custom_call_target="tpu_custom_call" | custom-call | tf_op jit(solution)/shard_map/routed_past/pallas_call | solution.py:280
  78.4 5.6 %collective-permute-done.14.rest_2_ = bf16[256,512]{1,0:T(8,128)(2,1)} collective-permute-done((bf16[256,512]{1,0:T(8,128)(2,1)}, bf16[256,512]{1,0:T(8,128)(2,1)}, u32[]{:S(2)}, u32[]{:S(2)}) %collective-permute-start.14) | collective-permute-done | bytes 262176 | tf_op jit(solution)/shard_map/ppermute | solution.py:134
  84.0 5.3 %collective-permute-done.11.wr1 = bf16[256,512]{1,0:T(8,128)(2,1)} collective-permute-done((bf16[256,512]{1,0:T(8,128)(2,1)S(1)}, bf16[256,512]{1,0:T(8,128)(2,1)}, u32[]{:S(2)}, u32[]{:S(2)}) %collective-permute-start.11) | collective-permute-done | bytes 262176 | tf_op jit(solution)/shard_map/ppermute | solution.py:134
  89.4 3.5 %project.3 = (bf16[256,1024]{1,0:T(8,128)(2,1)S(1)}, bf16[256,1024]{1,0:T(8,128)(2,1)}) custom-call(s32[4]{0:T(128)S(1)} %get-tuple-element.28.use, bf16[4,256,256]{2,1,0:T(8,128)(2,1)S(1)} %routed_past.1.routed, bf16[256,768]{1,0:T(8,128)(2,1)S(1)} %window_heads.1.l0, bf16[256,768]{1,0:T(8,128)(2,1)S(1)} %collective-permute-done.8.l1, ...), custom_call_target="tpu_custom_call" | custom-call | tf_op jit(solution)/shard_map/project/pallas_call | solution.py:384
  93.6 3.4 %project.2 = (bf16[256,1024]{1,0:T(8,128)(2,1)S(1)}, bf16[256,1024]{1,0:T(8,128)(2,1)}) custom-call(s32[4]{0:T(128)S(1)} %get-tuple-element.29.use, bf16[4,256,256]{2,1,0:T(8,128)(2,1)S(1)} %routed_past.1.routed, bf16[256,768]{1,0:T(8,128)(2,1)S(1)} %window_heads.1.l0, bf16[256,768]{1,0:T(8,128)(2,1)S(1)} %collective-permute-done.8.l1, ...), custom_call_target="tpu_custom_call" | custom-call | tf_op jit(solution)/shard_map/project/pallas_call | solution.py:384
  100.6 2.7 %collective-permute-start.19 = (bf16[256,512]{1,0:T(8,128)(2,1)S(1)}, bf16[256,512]{1,0:T(8,128)(2,1)S(1)}, u32[]{:S(2)}, u32[]{:S(2)}) collective-permute-start(bf16[256,512]{1,0:T(8,128)(2,1)S(1)} %get-tuple-element.23), channel_id=1, source_target_pairs={{0,8},{1,12},{2,10},{3,14},{4,0},{5,4},{6,2},{7,6},{8,1},{9,5},{10... | collective-permute-start | bytes 786440 | tf_op jit(solution)/shard_map/ppermute | solution.py:134
  103.3 3.4 %collective-permute-start.20 = (bf16[256,512]{1,0:T(8,128)(2,1)S(1)}, bf16[256,512]{1,0:T(8,128)(2,1)S(1)}, u32[]{:S(2)}, u32[]{:S(2)}) collective-permute-start(bf16[256,512]{1,0:T(8,128)(2,1)S(1)} %get-tuple-element.24), channel_id=1, source_target_pairs={{0,10},{1,14},{2,8},{3,12},{4,2},{5,6},{6,0},{7,4},{8,3},{9,7},{10... | collective-permute-start | bytes 786440 | tf_op jit(solution)/shard_map/ppermute | solution.py:134
  106.8 1.9 %collective-permute-start.16 = (bf16[256,512]{1,0:T(8,128)(2,1)S(1)}, bf16[256,512]{1,0:T(8,128)(2,1)S(1)}, u32[]{:S(2)}, u32[]{:S(2)}) collective-permute-start(bf16[256,512]{1,0:T(8,128)(2,1)S(1)} %get-tuple-element.19), channel_id=1, source_target_pairs={{0,0},{1,4},{2,2},{3,6},{4,8},{5,12},{6,10},{7,14},{8,9},{9,13},{1... | collective-permute-start | bytes 786440 | tf_op jit(solution)/shard_map/ppermute | solution.py:134
  108.9 1.9 %collective-permute-done.19.s1 = bf16[256,512]{1,0:T(8,128)(2,1)S(1)} collective-permute-done((bf16[256,512]{1,0:T(8,128)(2,1)S(1)}, bf16[256,512]{1,0:T(8,128)(2,1)S(1)}, u32[]{:S(2)}, u32[]{:S(2)}) %collective-permute-start.19) | collective-permute-done | bytes 262176 | tf_op jit(solution)/shard_map/ppermute | solution.py:134
  110.8 6.6 %collective-permute-done.20.c1 = bf16[256,512]{1,0:T(8,128)(2,1)S(1)} collective-permute-done((bf16[256,512]{1,0:T(8,128)(2,1)S(1)}, bf16[256,512]{1,0:T(8,128)(2,1)S(1)}, u32[]{:S(2)}, u32[]{:S(2)}) %collective-permute-start.20) | collective-permute-done | bytes 262176 | tf_op jit(solution)/shard_map/ppermute | solution.py:134
  118.8 4.4 %collective-permute-done.17.c0 = bf16[256,512]{1,0:T(8,128)(2,1)S(1)} collective-permute-done((bf16[256,512]{1,0:T(8,128)(2,1)S(1)}, bf16[256,512]{1,0:T(8,128)(2,1)S(1)}, u32[]{:S(2)}, u32[]{:S(2)}) %collective-permute-start.17) | collective-permute-done | bytes 262176 | tf_op jit(solution)/shard_map/ppermute | solution.py:134
  (68 shorter events, 13.7 us)
Async XLA Ops:
  2.2 40.0 %collective-permute-start.7 = (bf16[2,256,768]{2,1,0:T(8,128)(2,1)}, bf16[2,256,768]{2,1,0:T(8,128)(2,1)}, u32[]{:S(2)}, u32[]{:S(2)}) collective-permute-start(bf16[2,256,768]{2,1,0:T(8,128)(2,1)} %slice.16), channel_id=1, source_target_pairs={{0,4},{1,5},{2,6},{3,7},{4,8},{5,9},{6,10},{7,11},{8,12},{9,13},{1... | collective-permute-start | bytes 2359304 | tf_op jit(solution)/shard_map/ppermute | solution.py:134
  5.7 36.4 %copy-start.1 = (bf16[3,256,768]{2,1,0:T(8,128)(2,1)S(1)}, bf16[3,256,768]{2,1,0:T(8,128)(2,1)}, u32[]{:S(2)}) copy-start(bf16[3,256,768]{2,1,0:T(8,128)(2,1)} %qkv.1) | copy-start | bytes 3538948
  5.7 15.8 %collective-permute-start.3 = (bf16[528,256]{1,0:T(8,128)(2,1)S(1)}, bf16[528,256]{1,0:T(8,128)(2,1)}, u32[]{:S(2)}, u32[]{:S(2)}) collective-permute-start(bf16[528,256]{1,0:T(8,128)(2,1)S(1)} %slice.20), channel_id=1, source_target_pairs={{0,16},{1,17},{2,18},{3,19},{4,20},{5,21},{6,22},{7,23},{8,24},{9,... | collective-permute-start | bytes 811016 | tf_op jit(solution)/shard_map/ppermute | solution.py:134
  11.1 31.1 %collective-permute-start = (bf16[784,256]{1,0:T(8,128)(2,1)S(1)}, bf16[784,256]{1,0:T(8,128)(2,1)S(1)}, u32[]{:S(2)}, u32[]{:S(2)}) collective-permute-start(bf16[784,256]{1,0:T(8,128)(2,1)S(1)} %fusion.1.refs_0_), channel_id=1, source_target_pairs={{0,8},{1,9},{2,10},{3,11},{4,12},{5,13},{6,14},{7,15},{8,0},{9,1},... | collective-permute-start | bytes 1204232 | tf_op jit(solution)/shard_map/ppermute | solution.py:134
  21.5 26.6 %collective-permute-start.4 = (bf16[528,256]{1,0:T(8,128)(2,1)}, bf16[528,256]{1,0:T(8,128)(2,1)}, u32[]{:S(2)}, u32[]{:S(2)}) collective-permute-start(bf16[528,256]{1,0:T(8,128)(2,1)} %collective-permute-done.3.refs_4_), channel_id=1, source_target_pairs={{16,24},{17,25},{18,26},{19,27},{20,28},{21,29},{22,30},{23,31},{2... | collective-permute-start | bytes 811016 | tf_op jit(solution)/shard_map/ppermute | solution.py:134
  23.8 23.6 %collective-permute-start.12 = (bf16[256,512]{1,0:T(8,128)(2,1)}, bf16[256,512]{1,0:T(8,128)(2,1)}, u32[]{:S(2)}, u32[]{:S(2)}) collective-permute-start(bf16[256,512]{1,0:T(8,128)(2,1)} %get-tuple-element.27), channel_id=1, source_target_pairs={{0,16},{1,17},{2,18},{3,19},{4,20},{5,21},{6,22},{7,23},{8,24},{9,... | collective-permute-start | bytes 786440 | tf_op jit(solution)/shard_map/ppermute | solution.py:134
  27.9 24.5 %collective-permute-start.1 = (bf16[784,256]{1,0:T(8,128)(2,1)S(1)}, bf16[784,256]{1,0:T(8,128)(2,1)}, u32[]{:S(2)}, u32[]{:S(2)}) collective-permute-start(bf16[784,256]{1,0:T(8,128)(2,1)S(1)} %fusion.1.refs_0_), channel_id=1, source_target_pairs={{0,4},{1,5},{2,6},{3,7},{4,0},{5,1},{6,2},{7,3},{8,12},{9,13},{10,... | collective-permute-start | bytes 1204232 | tf_op jit(solution)/shard_map/ppermute | solution.py:134
  42.1 24.6 %collective-permute-start.2 = (bf16[784,256]{1,0:T(8,128)(2,1)S(1)}, bf16[784,256]{1,0:T(8,128)(2,1)}, u32[]{:S(2)}, u32[]{:S(2)}) collective-permute-start(bf16[784,256]{1,0:T(8,128)(2,1)S(1)} %collective-permute-done.refs_1_), channel_id=1, source_target_pairs={{0,4},{1,5},{2,6},{3,7},{4,0},{5,1},{6,2},{7,3},{8,12},{9,13},{10,... | collective-permute-start | bytes 1204232 | tf_op jit(solution)/shard_map/ppermute | solution.py:134
  42.2 27.5 %copy-start.13 = (s32[4]{0:T(128)S(1)}, s32[4]{0:T(128)}, u32[]{:S(2)}) copy-start(s32[4]{0:T(128)} %constant.112) | copy-start | bytes 52
  42.2 27.5 %copy-start.14 = (s32[4]{0:T(128)S(1)}, s32[4]{0:T(128)}, u32[]{:S(2)}) copy-start(s32[4]{0:T(128)} %constant.116) | copy-start | bytes 52
  45.4 23.9 %collective-permute-start.8 = (bf16[256,768]{1,0:T(8,128)(2,1)S(1)}, bf16[256,768]{1,0:T(8,128)(2,1)S(1)}, u32[]{:S(2)}, u32[]{:S(2)}) collective-permute-start(bf16[256,768]{1,0:T(8,128)(2,1)S(1)} %window_heads.1.l0), channel_id=1, source_target_pairs={{0,8},{1,9},{2,10},{3,11},{4,12},{5,13},{6,14},{7,15},{8,0},{9,1},... | collective-permute-start | bytes 1179656 | tf_op jit(solution)/shard_map/ppermute | solution.py:134
  47.4 12.7 %collective-permute-start.5 = (bf16[528,256]{1,0:T(8,128)(2,1)}, bf16[528,256]{1,0:T(8,128)(2,1)S(1)}, u32[]{:S(2)}, u32[]{:S(2)}) collective-permute-start(bf16[528,256]{1,0:T(8,128)(2,1)} %collective-permute-done.3.refs_4_), channel_id=1, source_target_pairs={{16,20},{17,21},{18,22},{19,23},{20,16},{21,17},{22,18},{23,19},{2... | collective-permute-start | bytes 811016 | tf_op jit(solution)/shard_map/ppermute | solution.py:134
  48.1 18.6 %collective-permute-start.6 = (bf16[528,256]{1,0:T(8,128)(2,1)}, bf16[528,256]{1,0:T(8,128)(2,1)S(1)}, u32[]{:S(2)}, u32[]{:S(2)}) collective-permute-start(bf16[528,256]{1,0:T(8,128)(2,1)} %collective-permute-done.4.refs_5_), channel_id=1, source_target_pairs={{16,20},{17,21},{18,22},{19,23},{20,16},{21,17},{22,18},{23,19},{2... | collective-permute-start | bytes 811016 | tf_op jit(solution)/shard_map/ppermute | solution.py:134
  52.4 26.1 %collective-permute-start.13 = (bf16[256,512]{1,0:T(8,128)(2,1)}, bf16[256,512]{1,0:T(8,128)(2,1)}, u32[]{:S(2)}, u32[]{:S(2)}) collective-permute-start(bf16[256,512]{1,0:T(8,128)(2,1)} %get-tuple-element.26), channel_id=1, source_target_pairs={{0,16},{1,17},{2,18},{3,19},{4,20},{5,21},{6,22},{7,23},{8,24},{9,... | collective-permute-start | bytes 786440 | tf_op jit(solution)/shard_map/ppermute | solution.py:134
  60.9 23.2 %collective-permute-start.14 = (bf16[256,512]{1,0:T(8,128)(2,1)}, bf16[256,512]{1,0:T(8,128)(2,1)}, u32[]{:S(2)}, u32[]{:S(2)}) collective-permute-start(bf16[256,512]{1,0:T(8,128)(2,1)} %get-tuple-element.25), channel_id=1, source_target_pairs={{0,16},{1,17},{2,18},{3,19},{4,20},{5,21},{6,22},{7,23},{8,24},{9,... | collective-permute-start | bytes 786440 | tf_op jit(solution)/shard_map/ppermute | solution.py:134
  66.7 22.7 %collective-permute-start.11 = (bf16[256,512]{1,0:T(8,128)(2,1)S(1)}, bf16[256,512]{1,0:T(8,128)(2,1)}, u32[]{:S(2)}, u32[]{:S(2)}) collective-permute-start(bf16[256,512]{1,0:T(8,128)(2,1)S(1)} %copy-done.2), channel_id=1, source_target_pairs={{0,16},{1,17},{2,18},{3,19},{4,20},{5,21},{6,22},{7,23},{8,24},{9,... | collective-permute-start | bytes 786440 | tf_op jit(solution)/shard_map/ppermute | solution.py:134
  67.5 21.9 %collective-permute-start.9 = (bf16[256,768]{1,0:T(8,128)(2,1)S(1)}, bf16[256,768]{1,0:T(8,128)(2,1)S(1)}, u32[]{:S(2)}, u32[]{:S(2)}) collective-permute-start(bf16[256,768]{1,0:T(8,128)(2,1)S(1)} %window_heads.1.l0), channel_id=1, source_target_pairs={{0,4},{1,5},{2,6},{3,7},{4,0},{5,1},{6,2},{7,3},{8,12},{9,13},{10,... | collective-permute-start | bytes 1179656 | tf_op jit(solution)/shard_map/ppermute | solution.py:134
  69.2 20.1 %collective-permute-start.10 = (bf16[256,768]{1,0:T(8,128)(2,1)S(1)}, bf16[256,768]{1,0:T(8,128)(2,1)S(1)}, u32[]{:S(2)}, u32[]{:S(2)}) collective-permute-start(bf16[256,768]{1,0:T(8,128)(2,1)S(1)} %collective-permute-done.8.l1), channel_id=1, source_target_pairs={{0,4},{1,5},{2,6},{3,7},{4,0},{5,1},{6,2},{7,3},{8,12},{9,13},{10,... | collective-permute-start | bytes 1179656 | tf_op jit(solution)/shard_map/ppermute | solution.py:134
  93.6 4.8 %collective-permute-start.18 = (bf16[256,1024]{1,0:T(8,128)(2,1)}, bf16[256,1024]{1,0:T(8,128)(2,1)}, u32[]{:S(2)}, u32[]{:S(2)}) collective-permute-start(bf16[256,1024]{1,0:T(8,128)(2,1)} %get-tuple-element.22), channel_id=1, source_target_pairs={{0,1},{1,0},{2,3},{3,2},{4,5},{5,4},{6,7},{7,6},{8,9},{9,8},{10,11... | collective-permute-start | bytes 1572872 | tf_op jit(solution)/shard_map/ppermute | solution.py:134
  97.9 8.8 %collective-permute-start.15 = (bf16[256,1024]{1,0:T(8,128)(2,1)}, bf16[256,1024]{1,0:T(8,128)(2,1)S(1)}, u32[]{:S(2)}, u32[]{:S(2)}) collective-permute-start(bf16[256,1024]{1,0:T(8,128)(2,1)} %get-tuple-element.18), channel_id=1, source_target_pairs={{0,1},{1,0},{2,3},{3,2},{4,5},{5,4},{6,7},{7,6},{8,9},{9,8},{10,11... | collective-permute-start | bytes 1572872 | tf_op jit(solution)/shard_map/ppermute | solution.py:134
  100.6 10.2 %collective-permute-start.19 = (bf16[256,512]{1,0:T(8,128)(2,1)S(1)}, bf16[256,512]{1,0:T(8,128)(2,1)S(1)}, u32[]{:S(2)}, u32[]{:S(2)}) collective-permute-start(bf16[256,512]{1,0:T(8,128)(2,1)S(1)} %get-tuple-element.23), channel_id=1, source_target_pairs={{0,8},{1,12},{2,10},{3,14},{4,0},{5,4},{6,2},{7,6},{8,1},{9,5},{10... | collective-permute-start | bytes 786440 | tf_op jit(solution)/shard_map/ppermute | solution.py:134
  103.3 14.1 %collective-permute-start.20 = (bf16[256,512]{1,0:T(8,128)(2,1)S(1)}, bf16[256,512]{1,0:T(8,128)(2,1)S(1)}, u32[]{:S(2)}, u32[]{:S(2)}) collective-permute-start(bf16[256,512]{1,0:T(8,128)(2,1)S(1)} %get-tuple-element.24), channel_id=1, source_target_pairs={{0,10},{1,14},{2,8},{3,12},{4,2},{5,6},{6,0},{7,4},{8,3},{9,7},{10... | collective-permute-start | bytes 786440 | tf_op jit(solution)/shard_map/ppermute | solution.py:134
  106.8 12.0 %collective-permute-start.16 = (bf16[256,512]{1,0:T(8,128)(2,1)S(1)}, bf16[256,512]{1,0:T(8,128)(2,1)S(1)}, u32[]{:S(2)}, u32[]{:S(2)}) collective-permute-start(bf16[256,512]{1,0:T(8,128)(2,1)S(1)} %get-tuple-element.19), channel_id=1, source_target_pairs={{0,0},{1,4},{2,2},{3,6},{4,8},{5,12},{6,10},{7,14},{8,9},{9,13},{1... | collective-permute-start | bytes 786440 | tf_op jit(solution)/shard_map/ppermute | solution.py:134
  108.8 14.4 %collective-permute-start.17 = (bf16[256,512]{1,0:T(8,128)(2,1)S(1)}, bf16[256,512]{1,0:T(8,128)(2,1)S(1)}, u32[]{:S(2)}, u32[]{:S(2)}) collective-permute-start(bf16[256,512]{1,0:T(8,128)(2,1)S(1)} %get-tuple-element.20), channel_id=1, source_target_pairs={{0,2},{1,6},{2,0},{3,4},{4,10},{5,14},{6,8},{7,12},{8,11},{9,15},{... | collective-permute-start | bytes 786440 | tf_op jit(solution)/shard_map/ppermute | solution.py:134
  (13 other events, 90.6 us)
